TPU v7x, 32 devices: a whole 2x2x4 slice. The times are simulated.
32 devices in a mesh: pairs: 2 (over x), band: 16 (over z, y, core).
Axes of the slice: x: 2, y: 2, z: 4, core: 2. Of those that a mesh axis runs over, the one named last changes fastest.
Arguments:
- query_tiles: bfloat16 [512, 256, 128], P(('pairs', 'band')), parts along dimension 0, may hold values from -52 to 52
- target: bfloat16 [512, 256, 128], P(('pairs', 'band')), parts along dimension 0, may hold values from -6 to 6
- tile_home: int32 [512], P('pairs'), parts along dimension 0, may hold values from 0 to 255, as said below
- candidates: int32 [512, 64], P(('pairs', 'band')), parts along dimension 0, may hold values from 0 to 255, as said below
- valid_mask: int32 [512, 64], P(('pairs', 'band')), parts along dimension 0, may hold values from 0 to 1, as said below
Outputs:
- matched: bfloat16 [512, 256, 128], P(('pairs', 'band')), parts along dimension 0
There are 2 independent parts, one for each index of `pairs`. A program takes and returns all parts, laid end to end along the dimension named above; each array names one. Nothing has to cross between parts.
Inputs may be any that keep to these rules, and one draw needn't show every extreme that they name: `tile_home`: a permutation of 0 to 255; target tile ids that agree modulo 16 are stored on the same device, storage row r lying on device r // 16. Ids in a row are distinct; the candidates of one device's query tiles all lie in one run of 128 consecutive ids taken modulo 256, and its first two query tiles together name every id of that run. `valid_mask`: the first entry of every row is 1.
All inputs are finite; a program needn't handle non-finite values.
Results may differ from a plain program's by a relative error of at most 0.0034.
Values may be sent and summed in bfloat16 or wider, within the bound.
No kernel may reach another device: no remote copies, remote signals or barrier semaphores. Data moves between devices by JAX's collectives and lax.ppermute only.
A program may use at most 128 MiB of HBM per device.

v0:
```python
import math
import jax
import jax.numpy as jnp
from jax import lax
from jax.sharding import PartitionSpec as P


def attend_tile(tile_query, tile_keys, keep_mask):
    per_tile = tile_keys.shape[0] // keep_mask.shape[0]
    scores = jnp.dot(tile_query, tile_keys.T, preferred_element_type=jnp.float32) * (
        1.0 / math.sqrt(tile_query.shape[1])
    )
    allowed = jnp.repeat(keep_mask > 0, per_tile)[None, :]
    scores = jnp.where(allowed, scores, -jnp.inf)
    peak = jnp.max(scores, axis=1, keepdims=True)
    raised = jnp.exp(scores - peak)
    totals = jnp.sum(raised, axis=1, keepdims=True)
    weights = (raised / totals).astype(jnp.bfloat16)
    return jnp.dot(weights, tile_keys, preferred_element_type=jnp.float32).astype(jnp.bfloat16)


def body(query_tiles, target, tile_home, candidates, valid_mask):
    channels = target.shape[2]
    stored_rows = tile_home[candidates]
    source = lax.all_gather(target, "band", axis=0, tiled=True)

    def one_tile(packed):
        tile_query, chosen, keep_mask = packed
        stored = source[chosen].reshape(-1, channels)
        return attend_tile(tile_query, stored, keep_mask)

    return lax.map(one_tile, (query_tiles, stored_rows, valid_mask))


def solution(mesh):
    in_specs = (
        P(("pairs", "band"), None, None),
        P(("pairs", "band"), None, None),
        P("pairs"),
        P(("pairs", "band"), None),
        P(("pairs", "band"), None),
    )
    out_specs = P(("pairs", "band"), None, None)
    return jax.shard_map(body, mesh=mesh, in_specs=in_specs, out_specs=out_specs, check_vma=False)
```

profile of v0, /device:TPU:0, one launch (start us, length us, event | category | flops | bytes accessed | tf_op | source)
XLA Modules:
  0.0 721.8 jit_solution(7972578319023650568)
XLA Ops:
  15.0 123.7 %all-gather.2.cloned.1.call-done = bf16[256,256,128]{2,1,0:T(8,128)(2,1)} async-done(((bf16[16,256,128]{2,1,0:T(8,128)(2,1)}), bf16[256,256,128]{2,1,0:T(8,128)(2,1)}) %all-gather.2.cloned.1.call-update) | async-done | bytes 16777232 | tf_op jit(solution)/shard_map/all_gather | solution.py:25
  138.7 575.3 %while.10 = (s32[]{:T(128)}, bf16[16,256,128]{2,1,0:T(8,128)(2,1)S(1)}, s32[16,64]{1,0:T(8,128)}, bf16[16,256,128]{2,1,0:T(8,128)(2,1)}, s32[16,64]{1,0:T(8,128)S(1)}, /*index=5*/bf16[256,256,128]{2,1,0:T(8,128)(2,1)}, s32[]{:T(128)}) while((s32[]{:T(128)}, bf16[16,256,128]{2,1,0:T(8,128)(2,1)S(1)}, s32[16,64]{1,0:T(8,128)}, ...), condition=%wide.region_3.4_spmd, body=%wide.region_0.3_spmd.sunk | while | flops 2181071616 | bytes 84093936 | solution.py:32
  148.4 10.4 %fusion.23 = (f32[256]{0:T(256)S(1)}, f32[256,16384]{1,0:T(8,128)}) fusion(bf16[16384,128]{1,0:T(8,128)(2,1)} %bitcast.38, bf16[16,256,128]{2,1,0:T(8,128)(2,1)} %get-tuple-element.110, s32[]{:T(128)} %get-tuple-element.100, pred[16384]{0:T(1024)(128)(4,1)S(1)} %broadcast_in_dim.37), kind=kOutput, calls=%fused_computation.23.clone.1 | convolution fusion | flops 1086324480 | bytes 21054976 | tf_op jit(solution)/shard_map/while/body/eval_jaxpr/dot_general | solution.py:10
  174.7 8.9 %gather_fusion = bf16[64,256,128]{2,1,0:T(8,128)(2,1)} fusion(bf16[256,256,128]{2,1,0:T(8,128)(2,1)} %get-tuple-element.112, s32[1024]{0:T(1024)S(1)} %pad_clamp_fusion.2), kind=kCustom, calls=%fused_computation.clone.1 | custom fusion | bytes 8388864 | tf_op jit(solution)/shard_map/while/body/eval_jaxpr/gather | solution.py:29
  184.4 10.4 %fusion.23 = (f32[256]{0:T(256)S(1)}, f32[256,16384]{1,0:T(8,128)}) fusion(bf16[16384,128]{1,0:T(8,128)(2,1)} %bitcast.38, bf16[16,256,128]{2,1,0:T(8,128)(2,1)} %get-tuple-element.110, s32[]{:T(128)} %get-tuple-element.100, pred[16384]{0:T(1024)(128)(4,1)S(1)} %broadcast_in_dim.37), kind=kOutput, calls=%fused_computation.23.clone.1 | convolution fusion | flops 1086324480 | bytes 21054976 | tf_op jit(solution)/shard_map/while/body/eval_jaxpr/dot_general | solution.py:10
  210.6 8.9 %gather_fusion = bf16[64,256,128]{2,1,0:T(8,128)(2,1)} fusion(bf16[256,256,128]{2,1,0:T(8,128)(2,1)} %get-tuple-element.112, s32[1024]{0:T(1024)S(1)} %pad_clamp_fusion.2), kind=kCustom, calls=%fused_computation.clone.1 | custom fusion | bytes 8388864 | tf_op jit(solution)/shard_map/while/body/eval_jaxpr/gather | solution.py:29
  220.3 10.4 %fusion.23 = (f32[256]{0:T(256)S(1)}, f32[256,16384]{1,0:T(8,128)}) fusion(bf16[16384,128]{1,0:T(8,128)(2,1)} %bitcast.38, bf16[16,256,128]{2,1,0:T(8,128)(2,1)} %get-tuple-element.110, s32[]{:T(128)} %get-tuple-element.100, pred[16384]{0:T(1024)(128)(4,1)S(1)} %broadcast_in_dim.37), kind=kOutput, calls=%fused_computation.23.clone.1 | convolution fusion | flops 1086324480 | bytes 21054976 | tf_op jit(solution)/shard_map/while/body/eval_jaxpr/dot_general | solution.py:10
  256.3 10.4 %fusion.23 = (f32[256]{0:T(256)S(1)}, f32[256,16384]{1,0:T(8,128)}) fusion(bf16[16384,128]{1,0:T(8,128)(2,1)} %bitcast.38, bf16[16,256,128]{2,1,0:T(8,128)(2,1)} %get-tuple-element.110, s32[]{:T(128)} %get-tuple-element.100, pred[16384]{0:T(1024)(128)(4,1)S(1)} %broadcast_in_dim.37), kind=kOutput, calls=%fused_computation.23.clone.1 | convolution fusion | flops 1086324480 | bytes 21054976 | tf_op jit(solution)/shard_map/while/body/eval_jaxpr/dot_general | solution.py:10
  282.5 8.9 %gather_fusion = bf16[64,256,128]{2,1,0:T(8,128)(2,1)} fusion(bf16[256,256,128]{2,1,0:T(8,128)(2,1)} %get-tuple-element.112, s32[1024]{0:T(1024)S(1)} %pad_clamp_fusion.2), kind=kCustom, calls=%fused_computation.clone.1 | custom fusion | bytes 8388864 | tf_op jit(solution)/shard_map/while/body/eval_jaxpr/gather | solution.py:29
  292.2 10.4 %fusion.23 = (f32[256]{0:T(256)S(1)}, f32[256,16384]{1,0:T(8,128)}) fusion(bf16[16384,128]{1,0:T(8,128)(2,1)} %bitcast.38, bf16[16,256,128]{2,1,0:T(8,128)(2,1)} %get-tuple-element.110, s32[]{:T(128)} %get-tuple-element.100, pred[16384]{0:T(1024)(128)(4,1)S(1)} %broadcast_in_dim.37), kind=kOutput, calls=%fused_computation.23.clone.1 | convolution fusion | flops 1086324480 | bytes 21054976 | tf_op jit(solution)/shard_map/while/body/eval_jaxpr/dot_general | solution.py:10
  328.2 10.4 %fusion.23 = (f32[256]{0:T(256)S(1)}, f32[256,16384]{1,0:T(8,128)}) fusion(bf16[16384,128]{1,0:T(8,128)(2,1)} %bitcast.38, bf16[16,256,128]{2,1,0:T(8,128)(2,1)} %get-tuple-element.110, s32[]{:T(128)} %get-tuple-element.100, pred[16384]{0:T(1024)(128)(4,1)S(1)} %broadcast_in_dim.37), kind=kOutput, calls=%fused_computation.23.clone.1 | convolution fusion | flops 1086324480 | bytes 21054976 | tf_op jit(solution)/shard_map/while/body/eval_jaxpr/dot_general | solution.py:10
  364.2 10.4 %fusion.23 = (f32[256]{0:T(256)S(1)}, f32[256,16384]{1,0:T(8,128)}) fusion(bf16[16384,128]{1,0:T(8,128)(2,1)} %bitcast.38, bf16[16,256,128]{2,1,0:T(8,128)(2,1)} %get-tuple-element.110, s32[]{:T(128)} %get-tuple-element.100, pred[16384]{0:T(1024)(128)(4,1)S(1)} %broadcast_in_dim.37), kind=kOutput, calls=%fused_computation.23.clone.1 | convolution fusion | flops 1086324480 | bytes 21054976 | tf_op jit(solution)/shard_map/while/body/eval_jaxpr/dot_general | solution.py:10
  400.1 10.4 %fusion.23 = (f32[256]{0:T(256)S(1)}, f32[256,16384]{1,0:T(8,128)}) fusion(bf16[16384,128]{1,0:T(8,128)(2,1)} %bitcast.38, bf16[16,256,128]{2,1,0:T(8,128)(2,1)} %get-tuple-element.110, s32[]{:T(128)} %get-tuple-element.100, pred[16384]{0:T(1024)(128)(4,1)S(1)} %broadcast_in_dim.37), kind=kOutput, calls=%fused_computation.23.clone.1 | convolution fusion | flops 1086324480 | bytes 21054976 | tf_op jit(solution)/shard_map/while/body/eval_jaxpr/dot_general | solution.py:10
  426.4 8.9 %gather_fusion = bf16[64,256,128]{2,1,0:T(8,128)(2,1)} fusion(bf16[256,256,128]{2,1,0:T(8,128)(2,1)} %get-tuple-element.112, s32[1024]{0:T(1024)S(1)} %pad_clamp_fusion.2), kind=kCustom, calls=%fused_computation.clone.1 | custom fusion | bytes 8388864 | tf_op jit(solution)/shard_map/while/body/eval_jaxpr/gather | solution.py:29
  436.1 10.4 %fusion.23 = (f32[256]{0:T(256)S(1)}, f32[256,16384]{1,0:T(8,128)}) fusion(bf16[16384,128]{1,0:T(8,128)(2,1)} %bitcast.38, bf16[16,256,128]{2,1,0:T(8,128)(2,1)} %get-tuple-element.110, s32[]{:T(128)} %get-tuple-element.100, pred[16384]{0:T(1024)(128)(4,1)S(1)} %broadcast_in_dim.37), kind=kOutput, calls=%fused_computation.23.clone.1 | convolution fusion | flops 1086324480 | bytes 21054976 | tf_op jit(solution)/shard_map/while/body/eval_jaxpr/dot_general | solution.py:10
  472.0 10.4 %fusion.23 = (f32[256]{0:T(256)S(1)}, f32[256,16384]{1,0:T(8,128)}) fusion(bf16[16384,128]{1,0:T(8,128)(2,1)} %bitcast.38, bf16[16,256,128]{2,1,0:T(8,128)(2,1)} %get-tuple-element.110, s32[]{:T(128)} %get-tuple-element.100, pred[16384]{0:T(1024)(128)(4,1)S(1)} %broadcast_in_dim.37), kind=kOutput, calls=%fused_computation.23.clone.1 | convolution fusion | flops 1086324480 | bytes 21054976 | tf_op jit(solution)/shard_map/while/body/eval_jaxpr/dot_general | solution.py:10
  508.0 10.4 %fusion.23 = (f32[256]{0:T(256)S(1)}, f32[256,16384]{1,0:T(8,128)}) fusion(bf16[16384,128]{1,0:T(8,128)(2,1)} %bitcast.38, bf16[16,256,128]{2,1,0:T(8,128)(2,1)} %get-tuple-element.110, s32[]{:T(128)} %get-tuple-element.100, pred[16384]{0:T(1024)(128)(4,1)S(1)} %broadcast_in_dim.37), kind=kOutput, calls=%fused_computation.23.clone.1 | convolution fusion | flops 1086324480 | bytes 21054976 | tf_op jit(solution)/shard_map/while/body/eval_jaxpr/dot_general | solution.py:10
  534.2 8.9 %gather_fusion = bf16[64,256,128]{2,1,0:T(8,128)(2,1)} fusion(bf16[256,256,128]{2,1,0:T(8,128)(2,1)} %get-tuple-element.112, s32[1024]{0:T(1024)S(1)} %pad_clamp_fusion.2), kind=kCustom, calls=%fused_computation.clone.1 | custom fusion | bytes 8388864 | tf_op jit(solution)/shard_map/while/body/eval_jaxpr/gather | solution.py:29
  544.0 10.4 %fusion.23 = (f32[256]{0:T(256)S(1)}, f32[256,16384]{1,0:T(8,128)}) fusion(bf16[16384,128]{1,0:T(8,128)(2,1)} %bitcast.38, bf16[16,256,128]{2,1,0:T(8,128)(2,1)} %get-tuple-element.110, s32[]{:T(128)} %get-tuple-element.100, pred[16384]{0:T(1024)(128)(4,1)S(1)} %broadcast_in_dim.37), kind=kOutput, calls=%fused_computation.23.clone.1 | convolution fusion | flops 1086324480 | bytes 21054976 | tf_op jit(solution)/shard_map/while/body/eval_jaxpr/dot_general | solution.py:10
  579.9 10.4 %fusion.23 = (f32[256]{0:T(256)S(1)}, f32[256,16384]{1,0:T(8,128)}) fusion(bf16[16384,128]{1,0:T(8,128)(2,1)} %bitcast.38, bf16[16,256,128]{2,1,0:T(8,128)(2,1)} %get-tuple-element.110, s32[]{:T(128)} %get-tuple-element.100, pred[16384]{0:T(1024)(128)(4,1)S(1)} %broadcast_in_dim.37), kind=kOutput, calls=%fused_computation.23.clone.1 | convolution fusion | flops 1086324480 | bytes 21054976 | tf_op jit(solution)/shard_map/while/body/eval_jaxpr/dot_general | solution.py:10
  615.9 10.4 %fusion.23 = (f32[256]{0:T(256)S(1)}, f32[256,16384]{1,0:T(8,128)}) fusion(bf16[16384,128]{1,0:T(8,128)(2,1)} %bitcast.38, bf16[16,256,128]{2,1,0:T(8,128)(2,1)} %get-tuple-element.110, s32[]{:T(128)} %get-tuple-element.100, pred[16384]{0:T(1024)(128)(4,1)S(1)} %broadcast_in_dim.37), kind=kOutput, calls=%fused_computation.23.clone.1 | convolution fusion | flops 1086324480 | bytes 21054976 | tf_op jit(solution)/shard_map/while/body/eval_jaxpr/dot_general | solution.py:10
  651.8 10.4 %fusion.23 = (f32[256]{0:T(256)S(1)}, f32[256,16384]{1,0:T(8,128)}) fusion(bf16[16384,128]{1,0:T(8,128)(2,1)} %bitcast.38, bf16[16,256,128]{2,1,0:T(8,128)(2,1)} %get-tuple-element.110, s32[]{:T(128)} %get-tuple-element.100, pred[16384]{0:T(1024)(128)(4,1)S(1)} %broadcast_in_dim.37), kind=kOutput, calls=%fused_computation.23.clone.1 | convolution fusion | flops 1086324480 | bytes 21054976 | tf_op jit(solution)/shard_map/while/body/eval_jaxpr/dot_general | solution.py:10
  678.1 8.9 %gather_fusion = bf16[64,256,128]{2,1,0:T(8,128)(2,1)} fusion(bf16[256,256,128]{2,1,0:T(8,128)(2,1)} %get-tuple-element.112, s32[1024]{0:T(1024)S(1)} %pad_clamp_fusion.2), kind=kCustom, calls=%fused_computation.clone.1 | custom fusion | bytes 8388864 | tf_op jit(solution)/shard_map/while/body/eval_jaxpr/gather | solution.py:29
  687.8 10.4 %fusion.23 = (f32[256]{0:T(256)S(1)}, f32[256,16384]{1,0:T(8,128)}) fusion(bf16[16384,128]{1,0:T(8,128)(2,1)} %bitcast.38, bf16[16,256,128]{2,1,0:T(8,128)(2,1)} %get-tuple-element.110, s32[]{:T(128)} %get-tuple-element.100, pred[16384]{0:T(1024)(128)(4,1)S(1)} %broadcast_in_dim.37), kind=kOutput, calls=%fused_computation.23.clone.1 | convolution fusion | flops 1086324480 | bytes 21054976 | tf_op jit(solution)/shard_map/while/body/eval_jaxpr/dot_general | solution.py:10
  (166 shorter events, 363.3 us)
Async XLA Ops:
  6.5 1.5 copy-start
  6.5 132.1 %all-gather.2.cloned.1.call-start = ((), (), s32[]{:S(2)}) async-start(), calls=%async_computation | async-start | bytes 17825792 | tf_op jit(solution)/shard_map/all_gather | solution.py:25
  148.4 18.6 %copy-start.1 = (bf16[64,256,128]{2,1,0:T(8,128)(2,1)S(1)}, bf16[64,256,128]{2,1,0:T(8,128)(2,1)}, u32[]{:S(2)}) copy-start(bf16[64,256,128]{2,1,0:T(8,128)(2,1)} %gather_fusion) | copy-start | bytes 12582916 | tf_op jit(solution)/shard_map/while
  184.4 18.6 %copy-start.1 = (bf16[64,256,128]{2,1,0:T(8,128)(2,1)S(1)}, bf16[64,256,128]{2,1,0:T(8,128)(2,1)}, u32[]{:S(2)}) copy-start(bf16[64,256,128]{2,1,0:T(8,128)(2,1)} %gather_fusion) | copy-start | bytes 12582916 | tf_op jit(solution)/shard_map/while
  220.3 18.6 %copy-start.1 = (bf16[64,256,128]{2,1,0:T(8,128)(2,1)S(1)}, bf16[64,256,128]{2,1,0:T(8,128)(2,1)}, u32[]{:S(2)}) copy-start(bf16[64,256,128]{2,1,0:T(8,128)(2,1)} %gather_fusion) | copy-start | bytes 12582916 | tf_op jit(solution)/shard_map/while
  256.3 18.6 %copy-start.1 = (bf16[64,256,128]{2,1,0:T(8,128)(2,1)S(1)}, bf16[64,256,128]{2,1,0:T(8,128)(2,1)}, u32[]{:S(2)}) copy-start(bf16[64,256,128]{2,1,0:T(8,128)(2,1)} %gather_fusion) | copy-start | bytes 12582916 | tf_op jit(solution)/shard_map/while
  292.2 18.6 %copy-start.1 = (bf16[64,256,128]{2,1,0:T(8,128)(2,1)S(1)}, bf16[64,256,128]{2,1,0:T(8,128)(2,1)}, u32[]{:S(2)}) copy-start(bf16[64,256,128]{2,1,0:T(8,128)(2,1)} %gather_fusion) | copy-start | bytes 12582916 | tf_op jit(solution)/shard_map/while
  328.2 18.6 %copy-start.1 = (bf16[64,256,128]{2,1,0:T(8,128)(2,1)S(1)}, bf16[64,256,128]{2,1,0:T(8,128)(2,1)}, u32[]{:S(2)}) copy-start(bf16[64,256,128]{2,1,0:T(8,128)(2,1)} %gather_fusion) | copy-start | bytes 12582916 | tf_op jit(solution)/shard_map/while
  364.2 18.6 %copy-start.1 = (bf16[64,256,128]{2,1,0:T(8,128)(2,1)S(1)}, bf16[64,256,128]{2,1,0:T(8,128)(2,1)}, u32[]{:S(2)}) copy-start(bf16[64,256,128]{2,1,0:T(8,128)(2,1)} %gather_fusion) | copy-start | bytes 12582916 | tf_op jit(solution)/shard_map/while
  400.1 18.6 %copy-start.1 = (bf16[64,256,128]{2,1,0:T(8,128)(2,1)S(1)}, bf16[64,256,128]{2,1,0:T(8,128)(2,1)}, u32[]{:S(2)}) copy-start(bf16[64,256,128]{2,1,0:T(8,128)(2,1)} %gather_fusion) | copy-start | bytes 12582916 | tf_op jit(solution)/shard_map/while
  436.1 18.6 %copy-start.1 = (bf16[64,256,128]{2,1,0:T(8,128)(2,1)S(1)}, bf16[64,256,128]{2,1,0:T(8,128)(2,1)}, u32[]{:S(2)}) copy-start(bf16[64,256,128]{2,1,0:T(8,128)(2,1)} %gather_fusion) | copy-start | bytes 12582916 | tf_op jit(solution)/shard_map/while
  472.0 18.6 %copy-start.1 = (bf16[64,256,128]{2,1,0:T(8,128)(2,1)S(1)}, bf16[64,256,128]{2,1,0:T(8,128)(2,1)}, u32[]{:S(2)}) copy-start(bf16[64,256,128]{2,1,0:T(8,128)(2,1)} %gather_fusion) | copy-start | bytes 12582916 | tf_op jit(solution)/shard_map/while
  508.0 18.6 %copy-start.1 = (bf16[64,256,128]{2,1,0:T(8,128)(2,1)S(1)}, bf16[64,256,128]{2,1,0:T(8,128)(2,1)}, u32[]{:S(2)}) copy-start(bf16[64,256,128]{2,1,0:T(8,128)(2,1)} %gather_fusion) | copy-start | bytes 12582916 | tf_op jit(solution)/shard_map/while
  543.9 18.6 %copy-start.1 = (bf16[64,256,128]{2,1,0:T(8,128)(2,1)S(1)}, bf16[64,256,128]{2,1,0:T(8,128)(2,1)}, u32[]{:S(2)}) copy-start(bf16[64,256,128]{2,1,0:T(8,128)(2,1)} %gather_fusion) | copy-start | bytes 12582916 | tf_op jit(solution)/shard_map/while
  579.9 18.6 %copy-start.1 = (bf16[64,256,128]{2,1,0:T(8,128)(2,1)S(1)}, bf16[64,256,128]{2,1,0:T(8,128)(2,1)}, u32[]{:S(2)}) copy-start(bf16[64,256,128]{2,1,0:T(8,128)(2,1)} %gather_fusion) | copy-start | bytes 12582916 | tf_op jit(solution)/shard_map/while
  615.9 18.6 %copy-start.1 = (bf16[64,256,128]{2,1,0:T(8,128)(2,1)S(1)}, bf16[64,256,128]{2,1,0:T(8,128)(2,1)}, u32[]{:S(2)}) copy-start(bf16[64,256,128]{2,1,0:T(8,128)(2,1)} %gather_fusion) | copy-start | bytes 12582916 | tf_op jit(solution)/shard_map/while
  651.8 18.6 %copy-start.1 = (bf16[64,256,128]{2,1,0:T(8,128)(2,1)S(1)}, bf16[64,256,128]{2,1,0:T(8,128)(2,1)}, u32[]{:S(2)}) copy-start(bf16[64,256,128]{2,1,0:T(8,128)(2,1)} %gather_fusion) | copy-start | bytes 12582916 | tf_op jit(solution)/shard_map/while
  687.8 18.6 %copy-start.1 = (bf16[64,256,128]{2,1,0:T(8,128)(2,1)S(1)}, bf16[64,256,128]{2,1,0:T(8,128)(2,1)}, u32[]{:S(2)}) copy-start(bf16[64,256,128]{2,1,0:T(8,128)(2,1)} %gather_fusion) | copy-start | bytes 12582916 | tf_op jit(solution)/shard_map/while
  714.0 1.0 copy-start.2
Sparse Core Ops, SparseCore 0:
  9.5 129.1 all-gather.1
where the time goes:
time: 724 us; the launch traced here: 722 us
  matrix products  289 us (40%)
  local copies, waits for them, and re-layouts  152 us (21%)
  other arithmetic  142 us (20%)
  waiting for transfers between devices  124 us (17%)
  between operations  13.4 us (2%)
    dot_general x16, matrix products, attend_tile(): jnp.dot(tile_query, tile_keys.T, preferred_element_type=jnp.float32)  167 us
    gather x16, local copies, waits for them, and re-layouts, one_tile(): stored = source[chosen].reshape(-1, channels)  142 us
    reduce_sum x16, other arithmetic, attend_tile(): totals = jnp.sum(raised, axis=1, keepdims=True)  130 us
    all_gather x1, waiting for transfers between devices, body(): source = lax.all_gather(target, 'band', axis=0, tiled=True)  124 us
    dot_general x16, matrix products, attend_tile(): jnp.dot(weights, tile_keys, preferred_element_type=jnp.float32)  122 us
  transfers between devices with their start and end apart: 1, of which 1 were waited for; matrix products, arithmetic and copies ran while one was open for 1% of the time, Pallas kernels for 0%

commit v1 on v0

--- a/solution.py
+++ b/solution.py
@@ -3,6 +3,13 @@
 import jax.numpy as jnp
 from jax import lax
 from jax.sharding import PartitionSpec as P
+from jax.lax import all_to_all, axis_size
+
+
+def solve_regions_on(original):
+    return jnp.concatenate(
+        all_to_all(jnp.stack(axis_size("band") * [original], 0), "band", 0, 0), 0
+    )
 
 
 def attend_tile(tile_query, tile_keys, keep_mask):
@@ -22,7 +29,7 @@
 def body(query_tiles, target, tile_home, candidates, valid_mask):
     channels = target.shape[2]
     stored_rows = tile_home[candidates]
-    source = lax.all_gather(target, "band", axis=0, tiled=True)
+    source = solve_regions_on(target)
 
     def one_tile(packed):
         tile_query, chosen, keep_mask = packed

time: 724 us -> 954 us (1.32)
  the two profiles are of different devices: /device:TPU:0 before, /device:TPU:13 now
where the time goes in v1:
time: 954 us; the launch traced here: 952 us
  waiting for transfers between devices  355 us (37%)
  matrix products  289 us (30%)
  local copies, waits for them, and re-layouts  159 us (17%)
  other arithmetic  142 us (15%)
    all_to_all x1, waiting for transfers between devices, solve_regions_on(): all_to_all(jnp.stack(axis_size('band') * [original], 0), 'band', 0, 0)  355 us
    dot_general x16, matrix products, attend_tile(): jnp.dot(tile_query, tile_keys.T, preferred_element_type=jnp.float32)  167 us
    gather x16, local copies, waits for them, and re-layouts, one_tile(): stored = source[chosen].reshape(-1, channels)  142 us
    reduce_sum x16, other arithmetic, attend_tile(): totals = jnp.sum(raised, axis=1, keepdims=True)  130 us
    dot_general x16, matrix products, attend_tile(): jnp.dot(weights, tile_keys, preferred_element_type=jnp.float32)  122 us
  transfers between devices with their start and end apart: 1, of which 1 were waited for; matrix products, arithmetic and copies ran while one was open for 1% of the time, Pallas kernels for 0%

profile of v1, /device:TPU:13, one launch (start us, length us, event | category | flops | bytes accessed | tf_op | source)
XLA Modules:
  0.0 952.1 jit_solution(10594737931668483883)
XLA Ops:
  20.8 355.1 %all-to-all-done = bf16[16,16,256,128]{3,2,1,0:T(8,128)(2,1)} async-done(((bf16[16,16,256,128]{3,2,1,0:T(8,128)(2,1)}), bf16[16,16,256,128]{3,2,1,0:T(8,128)(2,1)}, u32[]{:S(2)}, u32[]{:S(2)}) %all-to-all-start) | async-done | bytes 16777248 | tf_op jit(solution)/shard_map/all_to_all | solution.py:11
  375.9 575.3 %while.10 = (s32[]{:T(128)}, bf16[16,256,128]{2,1,0:T(8,128)(2,1)S(1)}, s32[16,64]{1,0:T(8,128)}, bf16[16,256,128]{2,1,0:T(8,128)(2,1)}, s32[16,64]{1,0:T(8,128)S(1)}, /*index=5*/bf16[256,256,128]{2,1,0:T(8,128)(2,1)}, s32[]{:T(128)}) while((s32[]{:T(128)}, bf16[16,256,128]{2,1,0:T(8,128)(2,1)S(1)}, s32[16,64]{1,0:T(8,128)}, ...), condition=%wide.region_3.4_spmd, body=%wide.region_0.3_spmd.sunk | while | flops 2181071616 | bytes 84093936 | solution.py:39
  385.6 10.4 %fusion.23 = (f32[256]{0:T(256)S(1)}, f32[256,16384]{1,0:T(8,128)}) fusion(bf16[16384,128]{1,0:T(8,128)(2,1)} %bitcast.39, bf16[16,256,128]{2,1,0:T(8,128)(2,1)} %get-tuple-element.110, s32[]{:T(128)} %get-tuple-element.100, pred[16384]{0:T(1024)(128)(4,1)S(1)} %broadcast_in_dim.37), kind=kOutput, calls=%fused_computation.23.clone.1 | convolution fusion | flops 1086324480 | bytes 21054976 | tf_op jit(solution)/shard_map/while/body/eval_jaxpr/dot_general | solution.py:17
  411.8 8.9 gather_fusion
  421.6 10.4 %fusion.23 = (f32[256]{0:T(256)S(1)}, f32[256,16384]{1,0:T(8,128)}) fusion(bf16[16384,128]{1,0:T(8,128)(2,1)} %bitcast.39, bf16[16,256,128]{2,1,0:T(8,128)(2,1)} %get-tuple-element.110, s32[]{:T(128)} %get-tuple-element.100, pred[16384]{0:T(1024)(128)(4,1)S(1)} %broadcast_in_dim.37), kind=kOutput, calls=%fused_computation.23.clone.1 | convolution fusion | flops 1086324480 | bytes 21054976 | tf_op jit(solution)/shard_map/while/body/eval_jaxpr/dot_general | solution.py:17
  447.8 8.9 gather_fusion
  457.5 10.4 %fusion.23 = (f32[256]{0:T(256)S(1)}, f32[256,16384]{1,0:T(8,128)}) fusion(bf16[16384,128]{1,0:T(8,128)(2,1)} %bitcast.39, bf16[16,256,128]{2,1,0:T(8,128)(2,1)} %get-tuple-element.110, s32[]{:T(128)} %get-tuple-element.100, pred[16384]{0:T(1024)(128)(4,1)S(1)} %broadcast_in_dim.37), kind=kOutput, calls=%fused_computation.23.clone.1 | convolution fusion | flops 1086324480 | bytes 21054976 | tf_op jit(solution)/shard_map/while/body/eval_jaxpr/dot_general | solution.py:17
  483.8 8.9 gather_fusion
  493.5 10.4 %fusion.23 = (f32[256]{0:T(256)S(1)}, f32[256,16384]{1,0:T(8,128)}) fusion(bf16[16384,128]{1,0:T(8,128)(2,1)} %bitcast.39, bf16[16,256,128]{2,1,0:T(8,128)(2,1)} %get-tuple-element.110, s32[]{:T(128)} %get-tuple-element.100, pred[16384]{0:T(1024)(128)(4,1)S(1)} %broadcast_in_dim.37), kind=kOutput, calls=%fused_computation.23.clone.1 | convolution fusion | flops 1086324480 | bytes 21054976 | tf_op jit(solution)/shard_map/while/body/eval_jaxpr/dot_general | solution.py:17
  529.4 10.4 %fusion.23 = (f32[256]{0:T(256)S(1)}, f32[256,16384]{1,0:T(8,128)}) fusion(bf16[16384,128]{1,0:T(8,128)(2,1)} %bitcast.39, bf16[16,256,128]{2,1,0:T(8,128)(2,1)} %get-tuple-element.110, s32[]{:T(128)} %get-tuple-element.100, pred[16384]{0:T(1024)(128)(4,1)S(1)} %broadcast_in_dim.37), kind=kOutput, calls=%fused_computation.23.clone.1 | convolution fusion | flops 1086324480 | bytes 21054976 | tf_op jit(solution)/shard_map/while/body/eval_jaxpr/dot_general | solution.py:17
  555.7 8.9 gather_fusion
  565.4 10.4 %fusion.23 = (f32[256]{0:T(256)S(1)}, f32[256,16384]{1,0:T(8,128)}) fusion(bf16[16384,128]{1,0:T(8,128)(2,1)} %bitcast.39, bf16[16,256,128]{2,1,0:T(8,128)(2,1)} %get-tuple-element.110, s32[]{:T(128)} %get-tuple-element.100, pred[16384]{0:T(1024)(128)(4,1)S(1)} %broadcast_in_dim.37), kind=kOutput, calls=%fused_computation.23.clone.1 | convolution fusion | flops 1086324480 | bytes 21054976 | tf_op jit(solution)/shard_map/while/body/eval_jaxpr/dot_general | solution.py:17
  601.3 10.4 %fusion.23 = (f32[256]{0:T(256)S(1)}, f32[256,16384]{1,0:T(8,128)}) fusion(bf16[16384,128]{1,0:T(8,128)(2,1)} %bitcast.39, bf16[16,256,128]{2,1,0:T(8,128)(2,1)} %get-tuple-element.110, s32[]{:T(128)} %get-tuple-element.100, pred[16384]{0:T(1024)(128)(4,1)S(1)} %broadcast_in_dim.37), kind=kOutput, calls=%fused_computation.23.clone.1 | convolution fusion | flops 1086324480 | bytes 21054976 | tf_op jit(solution)/shard_map/while/body/eval_jaxpr/dot_general | solution.py:17
  637.3 10.4 %fusion.23 = (f32[256]{0:T(256)S(1)}, f32[256,16384]{1,0:T(8,128)}) fusion(bf16[16384,128]{1,0:T(8,128)(2,1)} %bitcast.39, bf16[16,256,128]{2,1,0:T(8,128)(2,1)} %get-tuple-element.110, s32[]{:T(128)} %get-tuple-element.100, pred[16384]{0:T(1024)(128)(4,1)S(1)} %broadcast_in_dim.37), kind=kOutput, calls=%fused_computation.23.clone.1 | convolution fusion | flops 1086324480 | bytes 21054976 | tf_op jit(solution)/shard_map/while/body/eval_jaxpr/dot_general | solution.py:17
  663.5 8.9 gather_fusion
  673.3 10.4 %fusion.23 = (f32[256]{0:T(256)S(1)}, f32[256,16384]{1,0:T(8,128)}) fusion(bf16[16384,128]{1,0:T(8,128)(2,1)} %bitcast.39, bf16[16,256,128]{2,1,0:T(8,128)(2,1)} %get-tuple-element.110, s32[]{:T(128)} %get-tuple-element.100, pred[16384]{0:T(1024)(128)(4,1)S(1)} %broadcast_in_dim.37), kind=kOutput, calls=%fused_computation.23.clone.1 | convolution fusion | flops 1086324480 | bytes 21054976 | tf_op jit(solution)/shard_map/while/body/eval_jaxpr/dot_general | solution.py:17
  709.2 10.4 %fusion.23 = (f32[256]{0:T(256)S(1)}, f32[256,16384]{1,0:T(8,128)}) fusion(bf16[16384,128]{1,0:T(8,128)(2,1)} %bitcast.39, bf16[16,256,128]{2,1,0:T(8,128)(2,1)} %get-tuple-element.110, s32[]{:T(128)} %get-tuple-element.100, pred[16384]{0:T(1024)(128)(4,1)S(1)} %broadcast_in_dim.37), kind=kOutput, calls=%fused_computation.23.clone.1 | convolution fusion | flops 1086324480 | bytes 21054976 | tf_op jit(solution)/shard_map/while/body/eval_jaxpr/dot_general | solution.py:17
  745.2 10.4 %fusion.23 = (f32[256]{0:T(256)S(1)}, f32[256,16384]{1,0:T(8,128)}) fusion(bf16[16384,128]{1,0:T(8,128)(2,1)} %bitcast.39, bf16[16,256,128]{2,1,0:T(8,128)(2,1)} %get-tuple-element.110, s32[]{:T(128)} %get-tuple-element.100, pred[16384]{0:T(1024)(128)(4,1)S(1)} %broadcast_in_dim.37), kind=kOutput, calls=%fused_computation.23.clone.1 | convolution fusion | flops 1086324480 | bytes 21054976 | tf_op jit(solution)/shard_map/while/body/eval_jaxpr/dot_general | solution.py:17
  781.1 10.4 %fusion.23 = (f32[256]{0:T(256)S(1)}, f32[256,16384]{1,0:T(8,128)}) fusion(bf16[16384,128]{1,0:T(8,128)(2,1)} %bitcast.39, bf16[16,256,128]{2,1,0:T(8,128)(2,1)} %get-tuple-element.110, s32[]{:T(128)} %get-tuple-element.100, pred[16384]{0:T(1024)(128)(4,1)S(1)} %broadcast_in_dim.37), kind=kOutput, calls=%fused_computation.23.clone.1 | convolution fusion | flops 1086324480 | bytes 21054976 | tf_op jit(solution)/shard_map/while/body/eval_jaxpr/dot_general | solution.py:17
  807.4 8.9 gather_fusion
  817.1 10.4 %fusion.23 = (f32[256]{0:T(256)S(1)}, f32[256,16384]{1,0:T(8,128)}) fusion(bf16[16384,128]{1,0:T(8,128)(2,1)} %bitcast.39, bf16[16,256,128]{2,1,0:T(8,128)(2,1)} %get-tuple-element.110, s32[]{:T(128)} %get-tuple-element.100, pred[16384]{0:T(1024)(128)(4,1)S(1)} %broadcast_in_dim.37), kind=kOutput, calls=%fused_computation.23.clone.1 | convolution fusion | flops 1086324480 | bytes 21054976 | tf_op jit(solution)/shard_map/while/body/eval_jaxpr/dot_general | solution.py:17
  853.0 10.4 %fusion.23 = (f32[256]{0:T(256)S(1)}, f32[256,16384]{1,0:T(8,128)}) fusion(bf16[16384,128]{1,0:T(8,128)(2,1)} %bitcast.39, bf16[16,256,128]{2,1,0:T(8,128)(2,1)} %get-tuple-element.110, s32[]{:T(128)} %get-tuple-element.100, pred[16384]{0:T(1024)(128)(4,1)S(1)} %broadcast_in_dim.37), kind=kOutput, calls=%fused_computation.23.clone.1 | convolution fusion | flops 1086324480 | bytes 21054976 | tf_op jit(solution)/shard_map/while/body/eval_jaxpr/dot_general | solution.py:17
  889.0 10.4 %fusion.23 = (f32[256]{0:T(256)S(1)}, f32[256,16384]{1,0:T(8,128)}) fusion(bf16[16384,128]{1,0:T(8,128)(2,1)} %bitcast.39, bf16[16,256,128]{2,1,0:T(8,128)(2,1)} %get-tuple-element.110, s32[]{:T(128)} %get-tuple-element.100, pred[16384]{0:T(1024)(128)(4,1)S(1)} %broadcast_in_dim.37), kind=kOutput, calls=%fused_computation.23.clone.1 | convolution fusion | flops 1086324480 | bytes 21054976 | tf_op jit(solution)/shard_map/while/body/eval_jaxpr/dot_general | solution.py:17
  925.0 10.4 %fusion.23 = (f32[256]{0:T(256)S(1)}, f32[256,16384]{1,0:T(8,128)}) fusion(bf16[16384,128]{1,0:T(8,128)(2,1)} %bitcast.39, bf16[16,256,128]{2,1,0:T(8,128)(2,1)} %get-tuple-element.110, s32[]{:T(128)} %get-tuple-element.100, pred[16384]{0:T(1024)(128)(4,1)S(1)} %broadcast_in_dim.37), kind=kOutput, calls=%fused_computation.23.clone.1 | convolution fusion | flops 1086324480 | bytes 21054976 | tf_op jit(solution)/shard_map/while/body/eval_jaxpr/dot_general | solution.py:17
  (168 shorter events, 375.7 us)
Async XLA Ops:
  0.0 13.9 %copy-start = (s32[256]{0:T(256)S(1)}, s32[256]{0:T(256)}, u32[]{:S(2)}) copy-start(s32[256]{0:T(256)} %param.9) | copy-start | bytes 3076
  7.1 6.7 copy-start.2
  7.1 368.8 %all-to-all-start = ((bf16[16,16,256,128]{3,2,1,0:T(8,128)(2,1)}), bf16[16,16,256,128]{3,2,1,0:T(8,128)(2,1)}, u32[]{:S(2)}, u32[]{:S(2)}) async-start(bf16[16,16,256,128]{3,2,1,0:T(8,128)(2,1)} %stack.2), calls=%async_computation | async-start | bytes 33554432 | tf_op jit(solution)/shard_map/all_to_all | solution.py:11
  385.6 18.6 %copy-start.1 = (bf16[64,256,128]{2,1,0:T(8,128)(2,1)S(1)}, bf16[64,256,128]{2,1,0:T(8,128)(2,1)}, u32[]{:S(2)}) copy-start(bf16[64,256,128]{2,1,0:T(8,128)(2,1)} %gather_fusion) | copy-start | bytes 12582916 | tf_op jit(solution)/shard_map/while
  421.5 18.6 %copy-start.1 = (bf16[64,256,128]{2,1,0:T(8,128)(2,1)S(1)}, bf16[64,256,128]{2,1,0:T(8,128)(2,1)}, u32[]{:S(2)}) copy-start(bf16[64,256,128]{2,1,0:T(8,128)(2,1)} %gather_fusion) | copy-start | bytes 12582916 | tf_op jit(solution)/shard_map/while
  457.5 18.6 %copy-start.1 = (bf16[64,256,128]{2,1,0:T(8,128)(2,1)S(1)}, bf16[64,256,128]{2,1,0:T(8,128)(2,1)}, u32[]{:S(2)}) copy-start(bf16[64,256,128]{2,1,0:T(8,128)(2,1)} %gather_fusion) | copy-start | bytes 12582916 | tf_op jit(solution)/shard_map/while
  493.5 18.6 %copy-start.1 = (bf16[64,256,128]{2,1,0:T(8,128)(2,1)S(1)}, bf16[64,256,128]{2,1,0:T(8,128)(2,1)}, u32[]{:S(2)}) copy-start(bf16[64,256,128]{2,1,0:T(8,128)(2,1)} %gather_fusion) | copy-start | bytes 12582916 | tf_op jit(solution)/shard_map/while
  529.4 18.6 %copy-start.1 = (bf16[64,256,128]{2,1,0:T(8,128)(2,1)S(1)}, bf16[64,256,128]{2,1,0:T(8,128)(2,1)}, u32[]{:S(2)}) copy-start(bf16[64,256,128]{2,1,0:T(8,128)(2,1)} %gather_fusion) | copy-start | bytes 12582916 | tf_op jit(solution)/shard_map/while
  565.4 18.6 %copy-start.1 = (bf16[64,256,128]{2,1,0:T(8,128)(2,1)S(1)}, bf16[64,256,128]{2,1,0:T(8,128)(2,1)}, u32[]{:S(2)}) copy-start(bf16[64,256,128]{2,1,0:T(8,128)(2,1)} %gather_fusion) | copy-start | bytes 12582916 | tf_op jit(solution)/shard_map/while
  601.3 18.6 %copy-start.1 = (bf16[64,256,128]{2,1,0:T(8,128)(2,1)S(1)}, bf16[64,256,128]{2,1,0:T(8,128)(2,1)}, u32[]{:S(2)}) copy-start(bf16[64,256,128]{2,1,0:T(8,128)(2,1)} %gather_fusion) | copy-start | bytes 12582916 | tf_op jit(solution)/shard_map/while
  637.3 18.6 %copy-start.1 = (bf16[64,256,128]{2,1,0:T(8,128)(2,1)S(1)}, bf16[64,256,128]{2,1,0:T(8,128)(2,1)}, u32[]{:S(2)}) copy-start(bf16[64,256,128]{2,1,0:T(8,128)(2,1)} %gather_fusion) | copy-start | bytes 12582916 | tf_op jit(solution)/shard_map/while
  673.2 18.6 %copy-start.1 = (bf16[64,256,128]{2,1,0:T(8,128)(2,1)S(1)}, bf16[64,256,128]{2,1,0:T(8,128)(2,1)}, u32[]{:S(2)}) copy-start(bf16[64,256,128]{2,1,0:T(8,128)(2,1)} %gather_fusion) | copy-start | bytes 12582916 | tf_op jit(solution)/shard_map/while
  709.2 18.6 %copy-start.1 = (bf16[64,256,128]{2,1,0:T(8,128)(2,1)S(1)}, bf16[64,256,128]{2,1,0:T(8,128)(2,1)}, u32[]{:S(2)}) copy-start(bf16[64,256,128]{2,1,0:T(8,128)(2,1)} %gather_fusion) | copy-start | bytes 12582916 | tf_op jit(solution)/shard_map/while
  745.2 18.6 %copy-start.1 = (bf16[64,256,128]{2,1,0:T(8,128)(2,1)S(1)}, bf16[64,256,128]{2,1,0:T(8,128)(2,1)}, u32[]{:S(2)}) copy-start(bf16[64,256,128]{2,1,0:T(8,128)(2,1)} %gather_fusion) | copy-start | bytes 12582916 | tf_op jit(solution)/shard_map/while
  781.1 18.6 %copy-start.1 = (bf16[64,256,128]{2,1,0:T(8,128)(2,1)S(1)}, bf16[64,256,128]{2,1,0:T(8,128)(2,1)}, u32[]{:S(2)}) copy-start(bf16[64,256,128]{2,1,0:T(8,128)(2,1)} %gather_fusion) | copy-start | bytes 12582916 | tf_op jit(solution)/shard_map/while
  817.1 18.6 %copy-start.1 = (bf16[64,256,128]{2,1,0:T(8,128)(2,1)S(1)}, bf16[64,256,128]{2,1,0:T(8,128)(2,1)}, u32[]{:S(2)}) copy-start(bf16[64,256,128]{2,1,0:T(8,128)(2,1)} %gather_fusion) | copy-start | bytes 12582916 | tf_op jit(solution)/shard_map/while
  853.0 18.6 %copy-start.1 = (bf16[64,256,128]{2,1,0:T(8,128)(2,1)S(1)}, bf16[64,256,128]{2,1,0:T(8,128)(2,1)}, u32[]{:S(2)}) copy-start(bf16[64,256,128]{2,1,0:T(8,128)(2,1)} %gather_fusion) | copy-start | bytes 12582916 | tf_op jit(solution)/shard_map/while
  889.0 18.6 %copy-start.1 = (bf16[64,256,128]{2,1,0:T(8,128)(2,1)S(1)}, bf16[64,256,128]{2,1,0:T(8,128)(2,1)}, u32[]{:S(2)}) copy-start(bf16[64,256,128]{2,1,0:T(8,128)(2,1)} %gather_fusion) | copy-start | bytes 12582916 | tf_op jit(solution)/shard_map/while
  925.0 18.6 %copy-start.1 = (bf16[64,256,128]{2,1,0:T(8,128)(2,1)S(1)}, bf16[64,256,128]{2,1,0:T(8,128)(2,1)}, u32[]{:S(2)}) copy-start(bf16[64,256,128]{2,1,0:T(8,128)(2,1)} %gather_fusion) | copy-start | bytes 12582916 | tf_op jit(solution)/shard_map/while
  951.2 1.0 copy-start.3
